TPU v7x, 512 devices: a whole 4x4x16 slice. The times are simulated.
512 devices in a mesh: dp: 8 (over x_hi, y), fsdp: 64 (over z, x_lo, core).
Axes of the slice: x: 4 (x_hi: 2, x_lo: 2; x = x_hi * 2 + x_lo), y: 4, z: 16, core: 2. Of those that a mesh axis runs over, the one named last changes fastest.
Arguments:
- samples: bfloat16 [1024, 256, 768], P(('dp', 'fsdp')), may hold values from -6 to 6
- cotangent: bfloat16 [1024, 256, 768], P(('dp', 'fsdp')), may hold values from -6 to 6
- w_in: bfloat16 [3072, 768], P('fsdp'), may hold values from -0.21875 to 0.21875
- w_out: bfloat16 [3072, 768], P('fsdp'), may hold values from -0.21875 to 0.21875
- sketch_in: bfloat16 [768, 16], replicated, may hold values from -0.21875 to 0.21875
- sketch_hidden: bfloat16 [3072, 16], replicated, may hold values from -0.109375 to 0.109375
- targets: float32 [1024], P(('dp', 'fsdp')), may hold values from -6 to 6
Outputs:
- coeffs: float32 [1024], P(('dp', 'fsdp'))
- sketched_step: float32 [512], replicated
All inputs are finite; a program needn't handle non-finite values.
Results may differ from a plain program's by a relative error of at most 0.0054.
Values may be sent and summed in bfloat16 or wider, within the bound.
A program may use at most 64 MiB of HBM per device.

v0:
```python
import jax
import jax.numpy as jnp
from jax import lax
from jax.sharding import PartitionSpec as P

DAMPING = 0.5


def from_behind(value, axis, by):
    count = lax.axis_size(axis)
    return lax.ppermute(value, axis, [(i, (i + by) % count) for i in range(count)])


def per_device(samples, cotangent, w_in, w_out, sketch_in, sketch_hidden, targets):
    count, length, width = samples.shape
    flat_x = samples.reshape(count * length, width)
    flat_g = cotangent.reshape(count * length, width)
    rows_in = lax.all_gather(w_in, "fsdp", axis=0, tiled=True)
    rows_out = lax.all_gather(w_out, "fsdp", axis=0, tiled=True)
    pre = lax.dot_general(
        flat_x, rows_in, (((1,), (1,)), ((), ())), preferred_element_type=jnp.float32
    )
    back = lax.dot_general(
        flat_g, rows_out, (((1,), (1,)), ((), ())), preferred_element_type=jnp.float32
    )
    sig = jax.nn.sigmoid(pre)
    hidden = (pre * sig).astype(jnp.bfloat16)
    slope = (back * sig * (1.0 + pre * (1.0 - sig))).astype(jnp.bfloat16)
    hq = jnp.dot(hidden, sketch_hidden, preferred_element_type=jnp.float32)
    dq = jnp.dot(slope, sketch_hidden, preferred_element_type=jnp.float32)
    xp = jnp.dot(flat_x, sketch_in, preferred_element_type=jnp.float32)
    gp = jnp.dot(flat_g, sketch_in, preferred_element_type=jnp.float32)
    first = (
        jnp.einsum(
            "spr,spq->srq",
            dq.reshape(count, length, -1),
            xp.reshape(count, length, -1),
            precision=lax.Precision.HIGHEST,
        )
        / length
    )
    second = (
        jnp.einsum(
            "spr,spq->srq",
            hq.reshape(count, length, -1),
            gp.reshape(count, length, -1),
            precision=lax.Precision.HIGHEST,
        )
        / length
    )
    feats = jnp.concatenate([first.reshape(count, -1), second.reshape(count, -1)], axis=1).astype(
        jnp.bfloat16
    )
    feat_width = feats.shape[1]
    panel = lax.all_gather(feats, "fsdp", axis=0, tiled=True)
    all_targets = lax.all_gather(targets, ("dp", "fsdp"), axis=0, tiled=True)
    n_groups = lax.axis_size("dp")
    mine = lax.axis_index("dp")
    height = panel.shape[0]
    rows = jnp.zeros((height, height * n_groups), jnp.float32)
    collected = jnp.zeros((height * n_groups, feat_width), jnp.bfloat16)
    moving = panel
    for turn in range(n_groups):
        owner = (mine - turn) % n_groups
        block = lax.dot_general(
            panel, moving, (((1,), (1,)), ((), ())), preferred_element_type=jnp.float32
        )
        rows = lax.dynamic_update_slice_in_dim(rows, block, owner * height, 1)
        collected = lax.dynamic_update_slice_in_dim(collected, moving, owner * height, 0)
        if turn + 1 < n_groups:
            moving = from_behind(moving, "dp", 1)
    gram = lax.all_gather(rows, "dp", axis=0, tiled=True)
    total = gram.shape[0]
    factor = jnp.linalg.cholesky(gram + DAMPING * jnp.eye(total, dtype=jnp.float32))
    solved = jax.scipy.linalg.cho_solve((factor, True), all_targets)
    step = lax.dot_general(
        collected.astype(jnp.float32),
        solved,
        (((0,), (0,)), ((), ())),
        precision=lax.Precision.HIGHEST,
    )
    start = lax.axis_index(("dp", "fsdp")) * count
    coeffs = lax.dynamic_slice_in_dim(solved, start, count, 0)
    return (coeffs, step)


def solution(mesh):
    in_specs = (
        P(("dp", "fsdp"), None, None),
        P(("dp", "fsdp"), None, None),
        P("fsdp", None),
        P("fsdp", None),
        P(),
        P(),
        P(("dp", "fsdp")),
    )
    out_specs = (P(("dp", "fsdp")), P())
    return jax.shard_map(
        per_device, mesh=mesh, in_specs=in_specs, out_specs=out_specs, check_vma=False
    )
```

profile of v0, /device:TPU:1, one launch (start us, length us, event | category | flops | bytes accessed | tf_op | source)
XLA Modules:
  0.0 869.6 jit_solution(1005312438847361379)
XLA Ops:
  11.4 128.9 %all-gather.7.cloned.1.call-done = bf16[3072,768]{1,0:T(8,128)(2,1)} async-done(((bf16[48,768]{1,0:T(8,128)(2,1)}), bf16[3072,768]{1,0:T(8,128)(2,1)}) %all-gather.7.cloned.1.call-update) | async-done | bytes 4718608 | tf_op jit(solution)/shard_map/all_gather | solution.py:18
  140.3 4.6 fusion.134
  144.9 2.7 copy-done.6
  149.4 113.7 %all-gather.5.cloned.1.call-done = bf16[3072,768]{1,0:T(8,128)(2,1)} async-done(((bf16[48,768]{1,0:T(8,128)(2,1)}), bf16[3072,768]{1,0:T(8,128)(2,1)}) %all-gather.5.cloned.1.call-update) | async-done | bytes 4718608 | tf_op jit(solution)/shard_map/all_gather | solution.py:19
  263.1 8.0 fusion.2
  271.6 62.1 %all-gather = bf16[64,2,512]{2,1,0:T(2,128)(2,1)S(1)} all-gather(bf16[1,2,512]{2,1,0:T(2,128)(2,1)S(1)} %maximum_bitcast_fusion), channel_id=1, replica_groups=mesh['dp'=8,'fsdp'=64] {'fsdp'}, dimensions={0}, use_global_device_ids=true | all-gather | bytes 133120 | tf_op jit(solution)/shard_map/all_gather | solution.py:55
  333.8 3.1 collective-permute-start
  337.2 7.0 collective-permute-done
  346.3 7.2 collective-permute-done.1
  355.6 7.2 collective-permute-done.2
  364.9 7.2 collective-permute-done.3
  374.2 7.2 collective-permute-done.4
  383.6 7.2 collective-permute-done.5
  392.9 7.2 collective-permute-done.6
  401.4 106.3 %all-reduce.1 = f32[1024]{0:T(1024)S(1)} all-reduce(f32[1024]{0:T(1024)S(1)} %dynamic-update-slice.47), channel_id=1, replica_groups=mesh['dp'=8,'fsdp'=64] {'dp','fsdp'}, use_global_device_ids=true, to_apply=%add.1 | all-reduce | flops 1024 | bytes 8192
  507.9 4.8 select_add_fusion
  512.8 5.8 copy.14
  518.6 4.5 fusion
  525.0 11.7 %cholesky.222 = f32[128,128]{1,0:T(8,128)S(1)} custom-call(f32[128,128]{1,0:T(8,128)S(1)} %cholesky.577), custom_call_target="Cholesky" | custom-call | tf_op jit(solution)/shard_map/jit(cholesky)/cholesky | solution.py:74
  536.7 2.5 cholesky.254
  539.3 9.8 %custom-call.66 = f32[1,128,128]{1,2,0:T(8,128)S(1)} custom-call(f32[1,128,128]{2,1,0:T(8,128)S(1)} %get-tuple-element.41), custom_call_target="InvertDiagBlocksLowerTriangular" | custom-call | tf_op jit(solution)/shard_map/jit(cholesky)/cholesky | solution.py:74
  549.1 2.4 constant_dynamic-update-slice_fusion.51
  553.0 11.9 %cholesky.243 = f32[128,128]{1,0:T(8,128)S(1)} custom-call(f32[128,128]{1,0:T(8,128)S(1)} %cholesky.581), custom_call_target="Cholesky" | custom-call | tf_op jit(solution)/shard_map/jit(cholesky)/cholesky | solution.py:74
  565.5 9.8 %custom-call.67 = f32[1,128,128]{1,2,0:T(8,128)S(1)} custom-call(f32[1,128,128]{2,1,0:T(8,128)S(1)} %get-tuple-element.38), custom_call_target="InvertDiagBlocksLowerTriangular" | custom-call | tf_op jit(solution)/shard_map/jit(cholesky)/cholesky | solution.py:74
  578.7 11.7 %cholesky.466 = f32[128,128]{1,0:T(8,128)S(1)} custom-call(f32[128,128]{1,0:T(8,128)S(1)} %cholesky.586), custom_call_target="Cholesky" | custom-call | tf_op jit(solution)/shard_map/jit(cholesky)/cholesky | solution.py:74
  591.7 9.8 %custom-call.68 = f32[1,128,128]{1,2,0:T(8,128)S(1)} custom-call(f32[1,128,128]{2,1,0:T(8,128)S(1)} %get-tuple-element.35), custom_call_target="InvertDiagBlocksLowerTriangular" | custom-call | tf_op jit(solution)/shard_map/jit(cholesky)/cholesky | solution.py:74
  602.6 2.3 convolution_subtract_fusion.2
  605.0 11.9 %cholesky.485 = f32[128,128]{1,0:T(8,128)S(1)} custom-call(f32[128,128]{1,0:T(8,128)S(1)} %cholesky.591), custom_call_target="Cholesky" | custom-call | tf_op jit(solution)/shard_map/jit(cholesky)/cholesky | solution.py:74
  618.2 9.8 %custom-call.69 = f32[1,128,128]{1,2,0:T(8,128)S(1)} custom-call(f32[1,128,128]{2,1,0:T(8,128)S(1)} %get-tuple-element.32), custom_call_target="InvertDiagBlocksLowerTriangular" | custom-call | tf_op jit(solution)/shard_map/jit(cholesky)/cholesky | solution.py:74
  629.1 2.3 convolution_subtract_fusion.3
  631.5 11.7 %cholesky.504 = f32[128,128]{1,0:T(8,128)S(1)} custom-call(f32[128,128]{1,0:T(8,128)S(1)} %cholesky.596), custom_call_target="Cholesky" | custom-call | tf_op jit(solution)/shard_map/jit(cholesky)/cholesky | solution.py:74
  644.5 10.2 %custom-call.70 = f32[1,128,128]{1,2,0:T(8,128)S(1)} custom-call(f32[1,128,128]{2,1,0:T(8,128)S(1)} %get-tuple-element.29), custom_call_target="InvertDiagBlocksLowerTriangular" | custom-call | tf_op jit(solution)/shard_map/jit(cholesky)/cholesky | solution.py:74
  658.0 11.7 %cholesky.524 = f32[128,128]{1,0:T(8,128)S(1)} custom-call(f32[128,128]{1,0:T(8,128)S(1)} %cholesky.601), custom_call_target="Cholesky" | custom-call | tf_op jit(solution)/shard_map/jit(cholesky)/cholesky | solution.py:74
  671.0 9.8 %custom-call.71 = f32[1,128,128]{1,2,0:T(8,128)S(1)} custom-call(f32[1,128,128]{2,1,0:T(8,128)S(1)} %get-tuple-element.26), custom_call_target="InvertDiagBlocksLowerTriangular" | custom-call | tf_op jit(solution)/shard_map/jit(cholesky)/cholesky | solution.py:74
  683.8 11.9 %cholesky.544 = f32[128,128]{1,0:T(8,128)S(1)} custom-call(f32[128,128]{1,0:T(8,128)S(1)} %cholesky.606), custom_call_target="Cholesky" | custom-call | tf_op jit(solution)/shard_map/jit(cholesky)/cholesky | solution.py:74
  696.9 9.8 %custom-call.72 = f32[1,128,128]{1,2,0:T(8,128)S(1)} custom-call(f32[1,128,128]{2,1,0:T(8,128)S(1)} %get-tuple-element.23), custom_call_target="InvertDiagBlocksLowerTriangular" | custom-call | tf_op jit(solution)/shard_map/jit(cholesky)/cholesky | solution.py:74
  709.3 11.7 %cholesky.562 = f32[128,128]{1,0:T(8,128)S(1)} custom-call(f32[128,128]{1,0:T(8,128)S(1)} %slice_subtract_fusion), custom_call_target="Cholesky" | custom-call | tf_op jit(solution)/shard_map/jit(cholesky)/cholesky | solution.py:74
  727.9 4.8 select_select_fusion
  732.7 27.8 %while.1 = (s32[]{:T(128)}, f32[1024,1024]{1,0:T(8,128)}, s32[8,2]{0,1:T(2,128)S(1)}, f32[8,128,128]{2,1,0:T(8,128)}, s32[]{:T(128)}) while((s32[]{:T(128)}, f32[1024,1024]{1,0:T(8,128)}, s32[8,2]{0,1:T(2,128)S(1)}, f32[8,128,128]{2,1,0:T(8,128)}, s32[]{:T(128)}) %tuple.60), condition=%wide.while_cond, body=%wide.while_body.sunk | while | flops 2 | bytes 132705 | solution.py:75
  733.3 2.9 bitcast_dynamic-update-slice_fusion.2
  736.8 2.9 bitcast_dynamic-update-slice_fusion.2
  740.3 2.9 bitcast_dynamic-update-slice_fusion.2
  743.8 2.9 bitcast_dynamic-update-slice_fusion.2
  747.3 2.9 bitcast_dynamic-update-slice_fusion.2
  750.7 2.9 bitcast_dynamic-update-slice_fusion.2
  754.2 2.9 bitcast_dynamic-update-slice_fusion.2
  757.7 2.8 bitcast_dynamic-update-slice_fusion.2
  760.5 79.6 %custom-call.73 = f32[8,128,128]{1,2,0:T(8,128)S(1)} custom-call(f32[8,128,128]{2,1,0:T(8,128)} %get-tuple-element.9), custom_call_target="InvertDiagBlocksLowerTriangular" | custom-call | tf_op jit(solution)/shard_map/jit(_cho_solve)/triangular_solve | solution.py:75
  (161 shorter events, 75.1 us)
Async XLA Ops:
  7.2 1.7 copy-start
  7.2 133.1 %all-gather.7.cloned.1.call-start = ((), (), s32[]{:S(2)}) async-start(), calls=%async_computation.1 | async-start | bytes 4792320 | tf_op jit(solution)/shard_map/all_gather | solution.py:18
  7.9 255.2 %all-gather.5.cloned.1.call-start = ((), (), s32[]{:S(2)}) async-start(), calls=%async_computation | async-start | bytes 4792320 | tf_op jit(solution)/shard_map/all_gather | solution.py:19
  8.7 499.3 %all-gather.9.cloned.1.call-start = ((), (), s32[]{:S(2)}) async-start(), calls=%async_computation.2 | async-start | bytes 4718592 | tf_op jit(solution)/shard_map/all_gather | solution.py:72
  140.3 7.2 copy-start.4
  144.8 2.7 copy-start.6
  147.5 115.6 %copy-start.3 = (bf16[2,256,768]{2,1,0:T(8,128)(2,1)S(1)}, bf16[2,256,768]{2,1,0:T(8,128)(2,1)}, u32[]{:S(2)}) copy-start(bf16[2,256,768]{2,1,0:T(8,128)(2,1)} %param.8) | copy-start | bytes 2359300
  271.1 130.0 %copy-start.5 = (f32[2]{0:T(128)S(1)}, f32[2]{0:T(128)}, u32[]{:S(2)}) copy-start(f32[2]{0:T(128)} %param.13) | copy-start | bytes 28
  333.8 10.4 %collective-permute-start = (bf16[128,512]{1,0:T(8,128)(2,1)S(1)}, bf16[128,512]{1,0:T(8,128)(2,1)S(1)}, u32[]{:S(2)}, u32[]{:S(2)}) collective-permute-start(bf16[128,512]{1,0:T(8,128)(2,1)S(1)} %reshape.298), channel_id=1, source_target_pairs={{0,64},{64,128},{128,192},{192,256},{256,320},{320,384},{384,448},... | collective-permute-start | bytes 393224 | tf_op jit(solution)/shard_map/ppermute | solution.py:11
  344.2 9.3 %collective-permute-start.1 = (bf16[128,512]{1,0:T(8,128)(2,1)S(1)}, bf16[128,512]{1,0:T(8,128)(2,1)S(1)}, u32[]{:S(2)}, u32[]{:S(2)}) collective-permute-start(bf16[128,512]{1,0:T(8,128)(2,1)S(1)} %collective-permute-done), channel_id=1, source_target_pairs={{0,64},{64,128},{128,192},{192,256},{256,320},{320,384},{384,448},... | collective-permute-start | bytes 393224 | tf_op jit(solution)/shard_map/ppermute | solution.py:11
  353.5 9.3 %collective-permute-start.2 = (bf16[128,512]{1,0:T(8,128)(2,1)S(1)}, bf16[128,512]{1,0:T(8,128)(2,1)S(1)}, u32[]{:S(2)}, u32[]{:S(2)}) collective-permute-start(bf16[128,512]{1,0:T(8,128)(2,1)S(1)} %collective-permute-done.1), channel_id=1, source_target_pairs={{0,64},{64,128},{128,192},{192,256},{256,320},{320,384},{384,448},... | collective-permute-start | bytes 393224 | tf_op jit(solution)/shard_map/ppermute | solution.py:11
  362.8 9.3 %collective-permute-start.3 = (bf16[128,512]{1,0:T(8,128)(2,1)S(1)}, bf16[128,512]{1,0:T(8,128)(2,1)S(1)}, u32[]{:S(2)}, u32[]{:S(2)}) collective-permute-start(bf16[128,512]{1,0:T(8,128)(2,1)S(1)} %collective-permute-done.2), channel_id=1, source_target_pairs={{0,64},{64,128},{128,192},{192,256},{256,320},{320,384},{384,448},... | collective-permute-start | bytes 393224 | tf_op jit(solution)/shard_map/ppermute | solution.py:11
  372.1 9.3 %collective-permute-start.4 = (bf16[128,512]{1,0:T(8,128)(2,1)S(1)}, bf16[128,512]{1,0:T(8,128)(2,1)S(1)}, u32[]{:S(2)}, u32[]{:S(2)}) collective-permute-start(bf16[128,512]{1,0:T(8,128)(2,1)S(1)} %collective-permute-done.3), channel_id=1, source_target_pairs={{0,64},{64,128},{128,192},{192,256},{256,320},{320,384},{384,448},... | collective-permute-start | bytes 393224 | tf_op jit(solution)/shard_map/ppermute | solution.py:11
  381.4 9.3 %collective-permute-start.5 = (bf16[128,512]{1,0:T(8,128)(2,1)S(1)}, bf16[128,512]{1,0:T(8,128)(2,1)S(1)}, u32[]{:S(2)}, u32[]{:S(2)}) collective-permute-start(bf16[128,512]{1,0:T(8,128)(2,1)S(1)} %collective-permute-done.4), channel_id=1, source_target_pairs={{0,64},{64,128},{128,192},{192,256},{256,320},{320,384},{384,448},... | collective-permute-start | bytes 393224 | tf_op jit(solution)/shard_map/ppermute | solution.py:11
  390.8 9.3 %collective-permute-start.6 = (bf16[128,512]{1,0:T(8,128)(2,1)S(1)}, bf16[128,512]{1,0:T(8,128)(2,1)S(1)}, u32[]{:S(2)}, u32[]{:S(2)}) collective-permute-start(bf16[128,512]{1,0:T(8,128)(2,1)S(1)} %collective-permute-done.5), channel_id=1, source_target_pairs={{0,64},{64,128},{128,192},{192,256},{256,320},{320,384},{384,448},... | collective-permute-start | bytes 393224 | tf_op jit(solution)/shard_map/ppermute | solution.py:11
  400.3 0.8 copy-start.2
  523.1 1.9 copy-start.1
Sparse Core Ops, SparseCore 0:
  10.1 130.0 all-gather.6
  142.4 120.6 all-gather.4
  401.2 86.6 all-gather.8
where the time goes:
time: 878 us; the launch traced here: 870 us
  waiting for transfers between devices  294 us (33%)
  other arithmetic  266 us (30%)
  blocking collectives  168 us (19%)
  matrix products  63.4 us (7%)
  local copies, waits for them, and re-layouts  43.2 us (5%)
  between operations  19.6 us (2%)
  starting transfers between devices  14.7 us (2%)
    another operation x30, other arithmetic, per_device(): jnp.linalg.cholesky(gram + DAMPING * jnp.eye(total, dtype=jnp.float32))  172 us
    all_gather x1, waiting for transfers between devices, per_device(): rows_in = lax.all_gather(w_in, 'fsdp', axis=0, tiled=True)  129 us
    all_gather x1, waiting for transfers between devices, per_device(): rows_out = lax.all_gather(w_out, 'fsdp', axis=0, tiled=True)  114 us
    unnamed x1, blocking collectives  106 us
    another operation x3, other arithmetic, per_device(): solved = jax.scipy.linalg.cho_solve((factor, True), all_targets)  84.4 us
    all_gather x1, blocking collectives, per_device(): panel = lax.all_gather(feats, 'fsdp', axis=0, tiled=True)  62.1 us
    ppermute x7, waiting for transfers between devices, from_behind(): lax.ppermute(value, axis, [(i, (i + by) % count) for i in range(count)])  50.3 us
    another operation x24, local copies, waits for them, and re-layouts  27.8 us
  transfers between devices with their start and end apart: 10, of which 9 were waited for; matrix products, arithmetic and copies ran while one was open for 1% of the time, Pallas kernels for 0%

commit v1 on v0

v1 whole, which is shorter than its diff:
```python
import jax
import jax.numpy as jnp
from jax import lax
from jax.sharding import PartitionSpec as P

DAMPING = 0.5


def per_device(samples, cotangent, w_in, w_out, sketch_in, sketch_hidden, targets):
    count, length, width = samples.shape
    flat_x = samples.reshape(count * length, width)
    flat_g = cotangent.reshape(count * length, width)
    rows_in = lax.all_gather(w_in, "fsdp", axis=0, tiled=True)
    rows_out = lax.all_gather(w_out, "fsdp", axis=0, tiled=True)
    all_targets = lax.all_gather(targets, ("dp", "fsdp"), axis=0, tiled=True)
    pre = lax.dot_general(
        flat_x, rows_in, (((1,), (1,)), ((), ())), preferred_element_type=jnp.float32
    )
    back = lax.dot_general(
        flat_g, rows_out, (((1,), (1,)), ((), ())), preferred_element_type=jnp.float32
    )
    sig = jax.nn.sigmoid(pre)
    hidden = (pre * sig).astype(jnp.bfloat16)
    slope = (back * sig * (1.0 + pre * (1.0 - sig))).astype(jnp.bfloat16)
    hq = jnp.dot(hidden, sketch_hidden, preferred_element_type=jnp.float32)
    dq = jnp.dot(slope, sketch_hidden, preferred_element_type=jnp.float32)
    xp = jnp.dot(flat_x, sketch_in, preferred_element_type=jnp.float32)
    gp = jnp.dot(flat_g, sketch_in, preferred_element_type=jnp.float32)

    def outer(left, right):
        return (
            jnp.einsum(
                "spr,spq->srq",
                left.reshape(count, length, -1),
                right.reshape(count, length, -1),
                precision=lax.Precision.HIGHEST,
            )
            / length
        ).reshape(count, -1)

    feats = jnp.concatenate([outer(dq, xp), outer(hq, gp)], axis=1).astype(jnp.bfloat16)
    everyone = lax.all_gather(feats, ("dp", "fsdp"), axis=0, tiled=True)
    size = feats.shape[1]
    small = lax.dot_general(
        everyone, everyone, (((0,), (0,)), ((), ())), preferred_element_type=jnp.float32
    )
    right = lax.dot_general(
        everyone.astype(jnp.float32),
        all_targets,
        (((0,), (0,)), ((), ())),
        precision=lax.Precision.HIGHEST,
    )
    factor = jnp.linalg.cholesky(small + DAMPING * jnp.eye(size, dtype=jnp.float32))
    step = jax.scipy.linalg.cho_solve((factor, True), right)
    fitted = jnp.dot(feats.astype(jnp.float32), step, precision=lax.Precision.HIGHEST)
    coeffs = (targets - fitted) / DAMPING
    return (coeffs, step)


def solution(mesh):
    in_specs = (
        P(("dp", "fsdp"), None, None),
        P(("dp", "fsdp"), None, None),
        P("fsdp", None),
        P("fsdp", None),
        P(),
        P(),
        P(("dp", "fsdp")),
    )
    out_specs = (P(("dp", "fsdp")), P())
    return jax.shard_map(
        per_device, mesh=mesh, in_specs=in_specs, out_specs=out_specs, check_vma=False
    )
```

time: 878 us -> 1190 us (1.36)
  waiting for transfers between devices: 294 us -> 905 us
  other arithmetic: 266 us -> 118 us
  blocking collectives: 168 us -> 102 us
  matrix products: 63.4 us -> 28.8 us
  local copies, waits for them, and re-layouts: 43.2 us -> 15.5 us
  starting transfers between devices: 14.7 us -> 0.11 us
    all_gather x1, waiting for transfers between devices: 0.02 us -> 661 us  [per_device(): everyone = lax.all_gather(feats, ('dp', 'fsdp'), axis=0, tiled=True)]
    another operation x33 -> x18, other arithmetic: 257 us -> 118 us  [the longest x14 78.8 us: per_device(): jnp.linalg.cholesky(small + DAMPING * jnp.eye(size, dtype=jnp.float32))]
    all_gather x1 -> x0, blocking collectives: 62.1 us -> none  [per_device(): panel = lax.all_gather(feats, 'fsdp', axis=0, tiled=True)]
    ppermute x7 -> x0, waiting for transfers between devices: 50.3 us -> none  [from_behind(): lax.ppermute(value, axis, [(i, (i + by) % count) for i in range(count)])]
    another operation x44 -> x20, matrix products: 43.6 us -> 8.38 us  [the longest x6 5.46 us: per_device(): jnp.linalg.cholesky(small + DAMPING * jnp.eye(size, dtype=jnp.float32))]
    another operation x37 -> x17, local copies, waits for them, and re-layouts: 30.4 us -> 7.74 us
    ppermute x7 -> x0, starting transfers between devices: 14.6 us -> none  [from_behind(): lax.ppermute(value, axis, [(i, (i + by) % count) for i in range(count)])]
  transfers between devices with their start and end apart: 10 -> 3, of which waited for: 9 -> 3; matrix products, arithmetic and copies ran while one was open for 1% -> 1% of each run, Pallas kernels for 0% -> 0%
where the time goes in v1:
time: 1190 us
  waiting for transfers between devices  905 us (76%)
  other arithmetic  118 us (10%)
  blocking collectives  102 us (9%)
  matrix products  28.8 us (2%)
  between operations  16.5 us (1%)
  local copies, waits for them, and re-layouts  15.5 us (1%)
    all_gather x1, waiting for transfers between devices, per_device(): everyone = lax.all_gather(feats, ('dp', 'fsdp'), axis=0, tiled=True)  661 us
    all_gather x1, waiting for transfers between devices, per_device(): rows_in = lax.all_gather(w_in, 'fsdp', axis=0, tiled=True)  129 us
    all_gather x1, waiting for transfers between devices, per_device(): rows_out = lax.all_gather(w_out, 'fsdp', axis=0, tiled=True)  114 us
    unnamed x1, blocking collectives  102 us
    another operation x14, other arithmetic, per_device(): jnp.linalg.cholesky(small + DAMPING * jnp.eye(size, dtype=jnp.float32))  78.8 us
    another operation x4, other arithmetic, per_device(): step = jax.scipy.linalg.cho_solve((factor, True), right)  39.5 us
  transfers between devices with their start and end apart: 3, of which 3 were waited for; matrix products, arithmetic and copies ran while one was open for 1% of the time, Pallas kernels for 0%

profile of v1, /device:TPU:1, one launch (start us, length us, event | category | flops | bytes accessed | tf_op | source)
XLA Modules:
  0.0 1186.7 jit_solution(7681346825893043996)
XLA Ops:
  7.2 0.7 all-gather.7.cloned.1.call-update
  8.0 0.7 all-gather.5.cloned.1.call-update
  8.7 1.0 fusion.46
  9.8 1.5 fusion.44
  11.2 129.1 %all-gather.7.cloned.1.call-done = bf16[3072,768]{1,0:T(8,128)(2,1)} async-done(((bf16[48,768]{1,0:T(8,128)(2,1)}), bf16[3072,768]{1,0:T(8,128)(2,1)}) %all-gather.7.cloned.1.call-update) | async-done | bytes 4718608 | tf_op jit(solution)/shard_map/all_gather | solution.py:13
  140.3 4.6 fusion.74
  144.9 2.6 copy-done.9
  147.5 1.9 fusion
  149.4 113.7 %all-gather.5.cloned.1.call-done = bf16[3072,768]{1,0:T(8,128)(2,1)} async-done(((bf16[48,768]{1,0:T(8,128)(2,1)}), bf16[3072,768]{1,0:T(8,128)(2,1)}) %all-gather.5.cloned.1.call-update) | async-done | bytes 4718608 | tf_op jit(solution)/shard_map/all_gather | solution.py:14
  263.1 8.1 fusion.1
  271.7 0.6 copy-done.4
  272.4 0.2 dynamic-update-slice.23
  272.6 102.0 %all-reduce.1 = f32[1024]{0:T(1024)S(1)} all-reduce(f32[1024]{0:T(1024)S(1)} %dynamic-update-slice.23), channel_id=1, replica_groups=mesh['dp'=8,'fsdp'=64] {'dp','fsdp'}, use_global_device_ids=true, to_apply=%add.1 | all-reduce | flops 1024 | bytes 8192
  374.6 661.0 %all-gather.9.cloned.1.call-done = bf16[512,2,512]{2,1,0:T(2,128)(2,1)} async-done(((bf16[1,2,512]{2,1,0:T(2,128)(2,1)}), bf16[512,2,512]{2,1,0:T(2,128)(2,1)}) %all-gather.9.cloned.1.call-update) | async-done | bytes 1048592 | tf_op jit(solution)/shard_map/all_gather | solution.py:42
  1035.7 1.6 reshape.169
  1037.3 1.0 copy-done.1
  1038.3 0.7 fusion.75
  1039.0 0.3 copy.14
  1039.6 1.0 copy-done.2
  1040.7 11.7 cholesky.103
  1052.5 9.8 custom-call.34
  1062.4 1.2 constant_dynamic-update-slice_fusion.5
  1063.6 1.3 convolution_subtract_fusion
  1064.9 11.7 cholesky.215
  1076.6 10.0 custom-call.35
  1086.6 0.3 convolution_dynamic-update-slice_fusion
  1086.9 1.3 convolution_subtract_fusion.1
  1088.2 11.7 cholesky.236
  1099.9 0.7 compare_reduce_fusion.1
  1100.6 9.8 custom-call.36
  1110.6 1.2 convolution_subtract_fusion.2
  1111.9 11.9 %cholesky.253 = f32[128,128]{1,0:T(8,128)S(1)} custom-call(f32[128,128]{1,0:T(8,128)S(1)} %convolution_subtract_fusion.2), custom_call_target="Cholesky" | custom-call | tf_op jit(solution)/shard_map/jit(cholesky)/cholesky | solution.py:53
  1123.8 0.6 compare_reduce_fusion
  1124.4 0.7 compare_reduce_fusion.2
  1127.7 7.7 while.1
  1127.8 0.5 fusion.103
  1128.4 1.3 bitcast_dynamic-update-slice_fusion.2
  1129.7 0.5 fusion.103
  1130.3 1.3 bitcast_dynamic-update-slice_fusion.2
  1131.7 0.5 fusion.103
  1132.2 1.3 bitcast_dynamic-update-slice_fusion.2
  1133.6 0.5 fusion.103
  1134.1 1.3 bitcast_dynamic-update-slice_fusion.2
  1135.4 39.3 %custom-call.37 = f32[4,128,128]{1,2,0:T(8,128)S(1)} custom-call(f32[4,128,128]{2,1,0:T(8,128)S(1)} %get-tuple-element.9), custom_call_target="InvertDiagBlocksLowerTriangular" | custom-call | tf_op jit(solution)/shard_map/jit(_cho_solve)/triangular_solve | solution.py:54
  1174.7 1.7 fusion.76
  1177.4 0.3 fusion.15
  1178.9 0.3 fusion.13
  1179.5 0.6 fusion.17
  (58 shorter events, 4.3 us)
Async XLA Ops:
  7.2 1.5 copy-start
  7.2 133.1 %all-gather.7.cloned.1.call-start = ((), (), s32[]{:S(2)}) async-start(), calls=%async_computation.1 | async-start | bytes 4792320 | tf_op jit(solution)/shard_map/all_gather | solution.py:13
  7.9 255.2 %all-gather.5.cloned.1.call-start = ((), (), s32[]{:S(2)}) async-start(), calls=%async_computation | async-start | bytes 4792320 | tf_op jit(solution)/shard_map/all_gather | solution.py:14
  8.7 1027.0 %all-gather.9.cloned.1.call-start = ((), (), s32[]{:S(2)}) async-start(), calls=%async_computation.2 | async-start | bytes 1050624 | tf_op jit(solution)/shard_map/all_gather | solution.py:42
  140.3 7.2 copy-start.7
  144.8 2.7 copy-start.9
  147.5 115.6 %copy-start.3 = (bf16[2,256,768]{2,1,0:T(8,128)(2,1)S(1)}, bf16[2,256,768]{2,1,0:T(8,128)(2,1)}, u32[]{:S(2)}) copy-start(bf16[2,256,768]{2,1,0:T(8,128)(2,1)} %param.8) | copy-start | bytes 2359300
  263.1 9.3 copy-start.8
  271.7 0.6 copy-start.4
  1037.3 1.0 copy-start.1
  1039.4 140.1 %copy-start.5 = (bf16[2,512]{1,0:T(2,128)(2,1)S(1)}, bf16[2,512]{1,0:T(2,128)(2,1)}, u32[]{:S(2)}) copy-start(bf16[2,512]{1,0:T(2,128)(2,1)} %copy-done.4) | copy-start | bytes 6148
  1039.6 1.0 copy-start.2
  1179.5 0.7 copy-start.6
Sparse Core Ops, SparseCore 0:
  10.1 130.0 all-gather.6
  142.4 120.6 all-gather.4
  272.4 763.1 all-gather.8
